TPU v7x, 256 devices: a whole 4x4x8 slice. The times are simulated.
256 devices in a mesh: row: 32 (over z, x_lo, core), col: 8 (over y, x_hi).
Axes of the slice: x: 4 (x_hi: 2, x_lo: 2; x = x_hi * 2 + x_lo), y: 4, z: 8, core: 2. Of those that a mesh axis runs over, the one named last changes fastest.
Arguments:
- features: bfloat16 [32768, 440], P(('row', 'col')), may hold values from -1 to 1
- coeffs: bfloat16 [32768, 144], P(('row', 'col')), may hold values from -0.125 to 0.125
- targets: float32 [32768, 144], P(('row', 'col')), may hold values from -6 to 6
Outputs:
- residual: float32 [32768, 144], P(('row', 'col'))
All inputs are finite; a program needn't handle non-finite values.
Results may differ from a plain program's by a relative error of at most 0.0012.
Values may be sent and summed in bfloat16 or wider, within the bound.
A program may use at most 64 MiB of HBM per device.

v0:
```python
import jax
import jax.numpy as jnp
from jax import lax
from jax.sharding import PartitionSpec as P


def side_by_side(arrays, axis, dim, along):
    both = jnp.concatenate(arrays, axis=along)
    filled, at, finished = (lax.all_gather(both, axis, axis=dim, tiled=True), 0, [])
    for a in arrays:
        finished.append(lax.slice_in_dim(filled, at, at + a.shape[along], axis=along))
        at += a.shape[along]
    return tuple(finished)


def in_blocks(x, dim, size):
    shape = x.shape
    tiles = x.reshape(*shape[:dim], size, shape[dim] // size, *shape[dim + 1 :])
    return jnp.moveaxis(tiles, dim, 0)


def summed_on_arrival(x, axis, dim):
    size = lax.axis_size(axis)
    tiles = lax.all_to_all(in_blocks(x, dim, size), axis, 0, 0, tiled=True)
    return jnp.sum(tiles, axis=0)


def frame_squares(block):
    return jnp.sum(jnp.square(block.astype(jnp.float32)), axis=1)


def sweep(queries, keys, col_weights):
    rows = queries.shape[0]
    count = keys.shape[0]
    target = max(8, (1 << 20) // count)
    piece = rows
    while piece > target and piece % 2 == 0:
        piece = piece // 2
    steps = rows // piece
    key_squares = frame_squares(keys)
    query_squares = frame_squares(queries)
    query_blocks = queries.reshape(steps, piece, queries.shape[1])
    square_blocks = query_squares.reshape(steps, piece)

    def kernel_rows(query_part, square_part):
        inner = lax.dot_general(
            query_part, keys, (((1,), (1,)), ((), ())), preferred_element_type=jnp.float32
        )
        distance = jnp.sqrt(
            jnp.maximum(square_part[:, None] + key_squares[None, :] - 2.0 * inner, 0.0)
        )
        return jnp.exp(-distance).astype(jnp.bfloat16)

    def advance(carry, items):
        kernel = kernel_rows(items[0], items[1])
        return (carry, jnp.dot(kernel, col_weights, preferred_element_type=jnp.float32))

    unused, direct = lax.scan(advance, jnp.zeros((), jnp.float32), (query_blocks, square_blocks))
    return (direct.reshape(rows, col_weights.shape[1]), None)


def column_frames(features, coeffs):
    keys, weights = side_by_side((features, coeffs), "row", 0, 1)
    return (keys, weights)


def per_device(features, coeffs, targets):
    queries = lax.all_gather(features, "col", axis=0, tiled=True)
    keys, weights = column_frames(features, coeffs)
    direct, unused = sweep(queries, keys, weights)
    summed = summed_on_arrival(direct, "col", 0)
    return summed - targets


def solution(mesh):
    in_specs = (P(("row", "col"), None), P(("row", "col"), None), P(("row", "col"), None))
    out_specs = P(("row", "col"), None)
    return jax.shard_map(
        per_device, mesh=mesh, in_specs=in_specs, out_specs=out_specs, check_vma=False
    )
```

profile of v0, /device:TPU:1, one launch (start us, length us, event | category | flops | bytes accessed | tf_op | source)
XLA Modules:
  0.0 154.8 jit_solution(1261183756125022639)
XLA Ops:
  6.5 1.0 copy.11
  7.6 0.9 copy.12
  8.4 0.7 pad_maximum_fusion
  9.2 35.9 %all_gather.6 = bf16[1024,440]{0,1:T(8,128)(2,1)S(1)} all-gather(bf16[128,440]{0,1:T(8,128)(2,1)} %param.5), channel_id=1, replica_groups=mesh['row'=32,'col'=8] {'col'}, dimensions={0}, use_global_device_ids=true | all-gather | bytes 1013760 | tf_op jit(solution)/shard_map/all_gather | solution.py:68
  45.2 0.5 copy.13
  45.7 0.2 multiply_reduce_fusion.1
  45.9 36.4 %all-gather.2.cloned.1.call-done = bf16[4096,584]{1,0:T(8,128)(2,1)} async-done(((bf16[128,584]{1,0:T(8,128)(2,1)}), bf16[4096,584]{1,0:T(8,128)(2,1)}) %all-gather.2.cloned.1.call-update) | async-done | bytes 4784144 | tf_op jit(solution)/shard_map/all_gather | solution.py:9
  82.4 4.6 %slice.8 = bf16[4096,440]{1,0:T(8,128)(2,1)} slice(bf16[4096,584]{1,0:T(8,128)(2,1)} %all-gather.2.cloned.1.call-done), slice={[0:4096], [0:440]} | slice | bytes 7208960 | tf_op jit(solution)/shard_map/slice | solution.py:11
  87.0 1.0 slice.9
  88.0 1.0 multiply_reduce_fusion
  89.0 39.1 %while.10 = (s32[]{:T(128)}, f32[4,256,144]{1,0,2:T(4,128)}, f32[4,256]{1,0:T(4,128)S(1)}, f32[4096]{0:T(1024)S(1)}, bf16[4,256,440]{2,1,0:T(8,128)(2,1)S(1)}, /...) while((s32[]{:T(128)}, f32[4,256,144]{1,0,2:T(4,128)}, ...), condition=%wide.region_3.4_spmd, body=%wide.region_2.3_spmd.sunk | while | flops 1231028224 | bytes 6720617 | solution.py:58
  89.0 5.0 %fusion.25 = f32[1,256,144]{1,2,0:T(8,128)S(1)} fusion(bf16[4096,144]{1,0:T(8,128)(2,1)S(1)} %get-tuple-element.124, bf16[4096,440]{1,0:T(8,128)(2,1)} %get-tuple-element.123, f32[4096]{0:T(1024)S(1)} %get-tuple-element.121, f32[256]{0:T(256)S(1)} %bitcast.23, bf16[4,256,440]{2,1,0:T(8,128)(2,1)S(1)} %get-tuple-element.122, s32[]{:T(128)} %get-tuple-element.109), kind=kOutput, calls=%fused_computation.8.clone.1 | convolution fusion | flops 1231028224 | bytes 6128644 | tf_op jit(solution)/shard_map/while/body/eval_jaxpr/dot_general | solution.py:56
  94.1 0.2 copy.22
  94.2 4.6 %dynamic_update_slice.5 = f32[4,256,144]{1,0,2:T(4,128)} dynamic-update-slice(f32[4,256,144]{1,0,2:T(4,128)} %get-tuple-element.110, f32[1,256,144]{1,0,2:T(1,128)S(1)} %copy.22, s32[]{:T(128)} %get-tuple-element.109, s32[]{:T(128)} %constant.10.clone.1..sunk, s32[]{:T(128)} %constant.10.clone.1..sunk) | dynamic-update-slice | bytes 294916 | tf_op jit(solution)/shard_map/while/body/jit(dynamic_update_index_in_dim)/dynamic_update_slice | solution.py:58
  98.8 5.0 %fusion.25 = f32[1,256,144]{1,2,0:T(8,128)S(1)} fusion(bf16[4096,144]{1,0:T(8,128)(2,1)S(1)} %get-tuple-element.124, bf16[4096,440]{1,0:T(8,128)(2,1)} %get-tuple-element.123, f32[4096]{0:T(1024)S(1)} %get-tuple-element.121, f32[256]{0:T(256)S(1)} %bitcast.23, bf16[4,256,440]{2,1,0:T(8,128)(2,1)S(1)} %get-tuple-element.122, s32[]{:T(128)} %get-tuple-element.109), kind=kOutput, calls=%fused_computation.8.clone.1 | convolution fusion | flops 1231028224 | bytes 6128644 | tf_op jit(solution)/shard_map/while/body/eval_jaxpr/dot_general | solution.py:56
  103.8 0.2 copy.22
  104.0 4.6 %dynamic_update_slice.5 = f32[4,256,144]{1,0,2:T(4,128)} dynamic-update-slice(f32[4,256,144]{1,0,2:T(4,128)} %get-tuple-element.110, f32[1,256,144]{1,0,2:T(1,128)S(1)} %copy.22, s32[]{:T(128)} %get-tuple-element.109, s32[]{:T(128)} %constant.10.clone.1..sunk, s32[]{:T(128)} %constant.10.clone.1..sunk) | dynamic-update-slice | bytes 294916 | tf_op jit(solution)/shard_map/while/body/jit(dynamic_update_index_in_dim)/dynamic_update_slice | solution.py:58
  108.6 5.0 %fusion.25 = f32[1,256,144]{1,2,0:T(8,128)S(1)} fusion(bf16[4096,144]{1,0:T(8,128)(2,1)S(1)} %get-tuple-element.124, bf16[4096,440]{1,0:T(8,128)(2,1)} %get-tuple-element.123, f32[4096]{0:T(1024)S(1)} %get-tuple-element.121, f32[256]{0:T(256)S(1)} %bitcast.23, bf16[4,256,440]{2,1,0:T(8,128)(2,1)S(1)} %get-tuple-element.122, s32[]{:T(128)} %get-tuple-element.109), kind=kOutput, calls=%fused_computation.8.clone.1 | convolution fusion | flops 1231028224 | bytes 6128644 | tf_op jit(solution)/shard_map/while/body/eval_jaxpr/dot_general | solution.py:56
  113.8 4.6 %dynamic_update_slice.5 = f32[4,256,144]{1,0,2:T(4,128)} dynamic-update-slice(f32[4,256,144]{1,0,2:T(4,128)} %get-tuple-element.110, f32[1,256,144]{1,0,2:T(1,128)S(1)} %copy.22, s32[]{:T(128)} %get-tuple-element.109, s32[]{:T(128)} %constant.10.clone.1..sunk, s32[]{:T(128)} %constant.10.clone.1..sunk) | dynamic-update-slice | bytes 294916 | tf_op jit(solution)/shard_map/while/body/jit(dynamic_update_index_in_dim)/dynamic_update_slice | solution.py:58
  118.3 5.0 %fusion.25 = f32[1,256,144]{1,2,0:T(8,128)S(1)} fusion(bf16[4096,144]{1,0:T(8,128)(2,1)S(1)} %get-tuple-element.124, bf16[4096,440]{1,0:T(8,128)(2,1)} %get-tuple-element.123, f32[4096]{0:T(1024)S(1)} %get-tuple-element.121, f32[256]{0:T(256)S(1)} %bitcast.23, bf16[4,256,440]{2,1,0:T(8,128)(2,1)S(1)} %get-tuple-element.122, s32[]{:T(128)} %get-tuple-element.109), kind=kOutput, calls=%fused_computation.8.clone.1 | convolution fusion | flops 1231028224 | bytes 6128644 | tf_op jit(solution)/shard_map/while/body/eval_jaxpr/dot_general | solution.py:56
  123.5 4.6 %dynamic_update_slice.5 = f32[4,256,144]{1,0,2:T(4,128)} dynamic-update-slice(f32[4,256,144]{1,0,2:T(4,128)} %get-tuple-element.110, f32[1,256,144]{1,0,2:T(1,128)S(1)} %copy.22, s32[]{:T(128)} %get-tuple-element.109, s32[]{:T(128)} %constant.10.clone.1..sunk, s32[]{:T(128)} %constant.10.clone.1..sunk) | dynamic-update-slice | bytes 294916 | tf_op jit(solution)/shard_map/while/body/jit(dynamic_update_index_in_dim)/dynamic_update_slice | solution.py:58
  128.1 1.3 reshape_reshape.3
  129.5 17.8 %all_to_all.5 = f32[8,128,144]{1,2,0:T(8,128)S(1)} all-to-all(f32[8,128,144]{1,2,0:T(8,128)S(1)} %copy.15), channel_id=1, replica_groups=mesh['row'=32,'col'=8] {'col'}, dimensions={0} | all-to-all | bytes 1179648 | tf_op jit(solution)/shard_map/all_to_all | solution.py:24
  147.3 0.6 sub.6
  (16 shorter events, 0.5 us)
Async XLA Ops:
  6.5 75.8 %all-gather.2.cloned.1.call-start = ((), (), s32[]{:S(2)}) async-start(), calls=%async_computation.1 | async-start | bytes 5406720 | tf_op jit(solution)/shard_map/all_gather | solution.py:9
  82.4 4.6 %copy-start = (bf16[4096,584]{1,0:T(8,128)(2,1)S(1)}, bf16[4096,584]{1,0:T(8,128)(2,1)}, u32[]{:S(2)}) copy-start(bf16[4096,584]{1,0:T(8,128)(2,1)} %all-gather.2.cloned.1.call-done) | copy-start | bytes 14352388
  128.1 19.3 %copy-start.1 = (f32[128,144]{0,1:T(8,128)S(1)}, f32[128,144]{0,1:T(8,128)}, u32[]{:S(2)}) copy-start(f32[128,144]{0,1:T(8,128)} %param.7) | copy-start | bytes 221188
Sparse Core Ops, SparseCore 0:
  9.3 72.9 all-gather.1
where the time goes:
time: 156 us; the launch traced here: 155 us
  blocking collectives  53.7 us (34%)
  waiting for transfers between devices  36.5 us (23%)
  local copies, waits for them, and re-layouts  28.4 us (18%)
  matrix products  20.1 us (13%)
  between operations  13.5 us (9%)
  other arithmetic  2.6 us (2%)
    all_gather x1, waiting for transfers between devices, side_by_side(): lax.all_gather(both, axis, axis=dim, tiled=True)  36.4 us
    all_gather x1, blocking collectives, per_device(): queries = lax.all_gather(features, 'col', axis=0, tiled=True)  35.9 us
    dot_general x4, matrix products, advance(): jnp.dot(kernel, col_weights, preferred_element_type=jnp.float32)  20.1 us
    dynamic_update_slice x8, local copies, waits for them, and re-layouts, sweep(): lax.scan(advance, jnp.zeros((), jnp.float32), (query_blocks, square_blocks))  18.8 us
    all_to_all x1, blocking collectives, summed_on_arrival(): tiles = lax.all_to_all(in_blocks(x, dim, size), axis, 0, 0, tiled=True)  17.8 us
    slice x2, local copies, waits for them, and re-layouts, side_by_side(): lax.slice_in_dim(filled, at, at + a.shape[along], axis=along)  5.66 us
  transfers between devices with their start and end apart: 1, of which 1 were waited for; matrix products, arithmetic and copies ran while one was open for 0% of the time, Pallas kernels for 0%

commit v1 on v0

v1 whole, which is shorter than its diff:
```python
import functools

import jax
import jax.numpy as jnp
from jax import lax
from jax.experimental import pallas as pl
from jax.experimental.pallas import tpu as pltpu
from jax.sharding import PartitionSpec as P

MESH = pl.DeviceIdType.MESH
NX, NY, NZ = 4, 4, 8
FEAT, OUTS, OWN = 440, 144, 128
PAD = 512
WIRE = 448
HEAD = 64
PIECES = 5
LOG2E = 1.4426950408889634


def contract(a, b):
    return lax.dot_general(a, b, (((1,), (0,)), ((), ())), preferred_element_type=jnp.float32)


def laplacian(squared):
    squared = jnp.maximum(squared, 1e-30)
    return jnp.exp2((squared * -LOG2E) * lax.rsqrt(squared)).astype(jnp.bfloat16)


def kernel(
    feat_hbm, coef_hbm, out_ref,
    feat, coef, cols, weights, rows, gram, sent, inbox, own_sum,
    load_sem, z_send, z_recv, chip_send, chip_recv, p_send, q_send, relay_send, row_recv, out_send, out_recv,
):
    row, col = lax.axis_index("row"), lax.axis_index("col")
    z, core = row // 4, row % 2
    x, y = (col % 2) * 2 + (row // 2) % 2, col // 2
    flip = 1 - core

    def device(x, y, z, core):
        return (z * 4 + (x % 2) * 2 + core, y * 2 + x // 2)

    def plane(a, b):
        return device((x + flip * a + core * b) % NX, (y + core * a + flip * b) % NY, z, core)

    def line(step):
        return device(x, y, (z + step + NZ) % NZ, core)

    sibling = device(x, y, z, flip)

    barrier = pltpu.get_barrier_semaphore()
    near = [line(1), line(-1), sibling, plane(1, 0), plane(3, 0), plane(2, 0), plane(0, 1), plane(0, 3)]
    for peer in near:
        pl.semaphore_signal(barrier, inc=1, device_id=peer, device_id_type=MESH)

    load_feat = pltpu.make_async_copy(feat_hbm, feat, load_sem.at[0])
    load_coef = pltpu.make_async_copy(coef_hbm, coef, load_sem.at[1])
    load_feat.start()
    load_coef.start()

    @pl.loop(1, 16)
    def _(slot):
        rows[slot, WIRE:PAD, :] = jnp.zeros((PAD - WIRE, OWN), jnp.bfloat16)

    load_feat.wait()
    load_coef.wait()

    low = feat[:, 0:384].astype(jnp.float32)
    high = feat[:, 384:FEAT].astype(jnp.float32)
    square = jnp.sum(low * low, axis=1, keepdims=True) + jnp.sum(high * high, axis=1, keepdims=True)
    first = square.astype(jnp.bfloat16).astype(jnp.float32)
    second = (square - first).astype(jnp.bfloat16).astype(jnp.float32)
    third = square - first - second
    lane = lax.broadcasted_iota(jnp.int32, (OWN, 128), 1)
    high = jnp.concatenate([high, jnp.zeros((OWN, 128 - high.shape[1]), jnp.float32)], axis=1)
    coef_low = coef[:, 0:128].astype(jnp.float32)
    coef_high = jnp.concatenate([coef[:, 128:OUTS].astype(jnp.float32), jnp.zeros((OWN, 256 - OUTS), jnp.float32)], axis=1)
    pieces = jnp.where(lane % 3 == 2, first, jnp.where(lane % 3 == 0, second, third))
    ones = jnp.ones((OWN, 128), jnp.float32)
    nothing = jnp.zeros((OWN, 128), jnp.float32)
    column_tail = jnp.where(lane < 56, high * -2.0, jnp.where(lane < 59, pieces, jnp.where(lane < 62, ones, nothing)))
    column_tail = jnp.where(lane < 64, column_tail, pltpu.roll(coef_low, 64, 1))
    row_tail = jnp.where(lane < 56, high, jnp.where(lane < 59, ones, jnp.where(lane < 62, pieces, nothing)))
    cols[0, :, 0:384] = (low * -2.0).astype(jnp.bfloat16)
    cols[0, :, 384:PAD] = column_tail.astype(jnp.bfloat16)
    for t in range(3):
        rows[0, t * 128 : (t + 1) * 128, :] = jnp.transpose(low[:, t * 128 : (t + 1) * 128]).astype(jnp.bfloat16)
    rows[0, 384:PAD, :] = jnp.transpose(row_tail).astype(jnp.bfloat16)
    weights[0, 0:128, :] = jnp.transpose(coef_low).astype(jnp.bfloat16)
    weights[0, 128:OUTS, :] = jnp.transpose(coef_high)[0 : OUTS - 128].astype(jnp.bfloat16)

    pl.semaphore_wait(barrier, len(near))

    started = []

    def send(src, dst, send_sem, recv_sem, peer):
        copy = pltpu.make_async_remote_copy(
            src_ref=src, dst_ref=dst, send_sem=send_sem, recv_sem=recv_sem, device_id=peer, device_id_type=MESH
        )
        copy.start()
        started.append(copy)

    def arrived(dst, recv_sem):
        pltpu.make_async_remote_copy(
            src_ref=dst, dst_ref=dst, send_sem=load_sem.at[0], recv_sem=recv_sem, device_id=sibling, device_id_type=MESH
        ).wait_recv()

    def part(slot, piece):
        if piece < 4:
            return cols.at[slot, pl.ds(32 * piece, 32), :]
        return weights.at[slot, pl.ds(HEAD, OUTS - HEAD), :]

    def z_hop(step, piece, up):
        src = (8 - step + 1) % 8 if up else step - 1
        dst = 8 - step if up else step
        send(
            part(2 * src, piece), part(2 * dst, piece),
            z_send.at[int(up), step - 1, piece], z_recv.at[dst, piece], line(1 if up else -1),
        )

    def z_arrived(dz, piece):
        arrived(part(2 * dz, piece), z_recv.at[dz, piece])

    def to_sibling(dz):
        send(cols.at[2 * dz], cols.at[2 * dz + 1], chip_send.at[dz, 0], chip_recv.at[dz, 0], sibling)
        send(part(2 * dz, 4), part(2 * dz + 1, 4), chip_send.at[dz, 1], chip_recv.at[dz, 1], sibling)

    def from_sibling(dz):
        arrived(cols.at[2 * dz + 1], chip_recv.at[dz, 0])
        arrived(part(2 * dz + 1, 4), chip_recv.at[dz, 1])

    def row_block(a, b):
        return rows.at[4 * b + a, pl.ds(0, WIRE), :]

    def send_row(a, b, to_a, to_b, send_sem):
        there = ((a - to_a) % 4, (b - to_b) % 4)
        send(row_block(a, b), row_block(*there), send_sem, row_recv.at[4 * there[1] + there[0]], plane(to_a, to_b))

    def row_arrived(a, b):
        arrived(row_block(a, b), row_recv.at[4 * b + a])

    def across(a):
        send_row(a, 0, 0, 1, q_send.at[0, a])
        send_row(a, 0, 0, 3, q_send.at[1, a])

    def relay(a):
        if a < 2:
            row_arrived(a, 3)
            send_row(a, 3, 0, 1, relay_send.at[a])
        else:
            row_arrived(a, 1)
            send_row(a, 1, 0, 3, relay_send.at[a])

    def head_rows(slot):
        tail = jnp.transpose(cols[slot, :, 384:PAD].astype(jnp.float32))
        weights[slot, 0:HEAD, :] = tail[HEAD:128].astype(jnp.bfloat16)

    for piece in range(PIECES):
        for up in (True, False):
            z_hop(1, piece, up)
        if piece == 0:
            for a in (1, 3):
                send_row(0, 0, a, 0, p_send.at[a])
            across(0)
            send_row(0, 0, 2, 0, p_send.at[2])
    to_sibling(0)

    def z_round(step, pieces):
        for piece in pieces:
            for up in (True, False):
                z_arrived(8 - step if up else step, piece)
                if step < 3 or (step == 3 and (piece < 2) == up):
                    z_hop(step + 1, piece, up)

    z_round(1, (0, 1, 2))
    for a in (1, 3):
        row_arrived(a, 0)
        across(a)
    relay(0)
    z_round(1, (3, 4))
    to_sibling(1)
    to_sibling(7)
    row_arrived(2, 0)
    across(2)
    z_round(2, (0, 1))
    relay(1)
    relay(3)
    z_round(2, (2, 3, 4))
    to_sibling(2)
    to_sibling(6)
    relay(2)
    from_sibling(0)
    for dz in (1, 7):
        from_sibling(dz)
        head_rows(2 * dz)
        head_rows(2 * dz + 1)
    head_rows(1)
    z_round(3, range(5))
    to_sibling(3)
    to_sibling(5)
    for dz in (2, 6):
        from_sibling(dz)
        head_rows(2 * dz)
        head_rows(2 * dz + 1)
    for piece in range(5):
        z_arrived(4, piece)
    to_sibling(4)
    for dz in (3, 5, 4):
        head_rows(2 * dz)
        from_sibling(dz)
        head_rows(2 * dz + 1)
    for a, b in ((0, 1), (1, 1), (3, 3), (2, 3), (0, 2), (1, 2), (2, 2), (3, 2)):
        row_arrived(a, b)

    all_weights = jnp.concatenate([weights[slot] for slot in range(16)], axis=1)

    def out_copy(a, b):
        slot = 4 * b + a
        return pltpu.make_async_remote_copy(
            src_ref=sent.at[slot], dst_ref=inbox.at[slot], send_sem=out_send.at[slot], recv_sem=out_recv.at[slot],
            device_id=plane(a, b), device_id_type=MESH,
        )

    @pl.loop(0, 4)
    def _(b):
        group = jnp.concatenate([rows[4 * b + a] for a in range(4)], axis=1)
        for slot in range(0, 16, 2):
            block = cols[slot : slot + 2].reshape(2 * OWN, PAD)
            gram[slot * OWN : (slot + 2) * OWN, :] = laplacian(contract(block, group))
        total = contract(all_weights, gram[...])

        @pl.when(b == 0)
        def _():
            own_sum[...] = total[:, 0:OWN]

        for a in range(4):
            sent[4 * b + a] = total[:, a * OWN : (a + 1) * OWN].astype(jnp.bfloat16)
        for a in range(4):
            if a == 0:
                @pl.when(b > 0)
                def _():
                    out_copy(0, b).start()
            else:
                out_copy(a, b).start()

    total = own_sum[...]
    for slot in range(1, 16):
        arrived(inbox.at[slot], out_recv.at[slot])
        total = total + inbox[slot].astype(jnp.float32)
    out_ref[:, 0:128] = jnp.transpose(total[0:128])
    rest = jnp.concatenate([total[128:OUTS], jnp.zeros((256 - OUTS, OWN), jnp.float32)], axis=0)
    out_ref[:, 128:OUTS] = jnp.transpose(rest)[:, 0 : OUTS - 128]

    for copy in started:
        copy.wait_send()
    for slot in range(1, 16):
        out_copy(slot % 4, slot // 4).wait_send()


def per_device(features, coeffs, targets):
    dma = pltpu.SemaphoreType.DMA
    predicted = pl.pallas_call(
        kernel,
        out_shape=jax.ShapeDtypeStruct((OWN, OUTS), jnp.float32),
        in_specs=[pl.BlockSpec(memory_space=pl.ANY)] * 2,
        out_specs=pl.BlockSpec(memory_space=pltpu.VMEM),
        scratch_shapes=[
            pltpu.VMEM((OWN, FEAT), jnp.bfloat16),
            pltpu.VMEM((OWN, OUTS), jnp.bfloat16),
            pltpu.VMEM((16, OWN, PAD), jnp.bfloat16),
            pltpu.VMEM((16, OUTS, OWN), jnp.bfloat16),
            pltpu.VMEM((16, PAD, OWN), jnp.bfloat16),
            pltpu.VMEM((16 * OWN, 4 * OWN), jnp.bfloat16),
            pltpu.VMEM((16, OUTS, OWN), jnp.bfloat16),
            pltpu.VMEM((16, OUTS, OWN), jnp.bfloat16),
            pltpu.VMEM((OUTS, OWN), jnp.float32),
            dma((2,)),
            dma((2, 4, PIECES)), dma((8, PIECES)),
            dma((8, 2)), dma((8, 2)),
            dma((4,)), dma((2, 4)), dma((4,)), dma((16,)),
            dma((16,)), dma((16,)),
        ],
        compiler_params=pltpu.CompilerParams(collective_id=0, has_side_effects=True, vmem_limit_bytes=48 << 20),
        name="ridge",
    )(features, coeffs)
    return predicted - targets


def solution(mesh):
    spec = P(("row", "col"), None)
    return jax.shard_map(per_device, mesh=mesh, in_specs=(spec, spec, spec), out_specs=spec, check_vma=False)
```

time: 156 us -> 45.3 us (0.29)
  blocking collectives: 53.7 us -> 0 us
  Pallas kernels: 0 us -> 42.3 us
  waiting for transfers between devices: 36.5 us -> 0 us
  local copies, waits for them, and re-layouts: 28.4 us -> 2.73 us
  matrix products: 20.1 us -> 0 us
  between operations: 13.5 us -> 0.06 us
  other arithmetic: 2.6 us -> 0.02 us
    pallas_call x0 -> x1, Pallas kernels: none -> 42.3 us  [per_device(): pl.pallas_call(kernel, out_shape=jax.ShapeDtypeStruct((OWN, OUTS), jnp.fl...]
    all_gather x1 -> x0, waiting for transfers between devices: 36.4 us -> none  [side_by_side(): lax.all_gather(both, axis, axis=dim, tiled=True)]
    all_gather x1 -> x0, blocking collectives: 35.9 us -> none  [per_device(): queries = lax.all_gather(features, 'col', axis=0, tiled=True)]
    dot_general x4 -> x0, matrix products: 20.1 us -> none  [advance(): jnp.dot(kernel, col_weights, preferred_element_type=jnp.float32)]
    dynamic_update_slice x8 -> x0, local copies, waits for them, and re-layouts: 18.8 us -> none  [sweep(): lax.scan(advance, jnp.zeros((), jnp.float32), (query_blocks, square_blocks))]
    all_to_all x1 -> x0, blocking collectives: 17.8 us -> none  [summed_on_arrival(): tiles = lax.all_to_all(in_blocks(x, dim, size), axis, 0, 0, tiled=True)]
    slice x2 -> x0, local copies, waits for them, and re-layouts: 5.66 us -> none  [side_by_side(): lax.slice_in_dim(filled, at, at + a.shape[along], axis=along)]
  transfers between devices with their start and end apart: 1 -> 0, of which waited for: 1 -> 0; matrix products, arithmetic and copies ran while one was open for 0% -> 0% of each run, Pallas kernels for 0% -> 0%
where the time goes in v1:
time: 45.3 us; the launch traced here: 45.1 us
  Pallas kernels  42.3 us (93%)
  local copies, waits for them, and re-layouts  2.73 us (6%)
    pallas_call x1, Pallas kernels, per_device(): pl.pallas_call(kernel, out_shape=jax.ShapeDtypeStruct((OWN, OUTS), jnp.fl...  42.3 us
    unnamed x5, local copies, waits for them, and re-layouts  2 us

profile of v1, /device:TPU:1, one launch (start us, length us, event | category | flops | bytes accessed | tf_op | source)
XLA Modules:
  0.0 45.1 jit_solution(77669383471441380)
XLA Ops:
  0.0 0.9 %copy.9.coef_hbm = bf16[128,144]{1,0:T(8,128)(2,1)S(1)} copy(bf16[128,144]{0,1:T(8,128)(2,1)} %param.4) | data formatting | bytes 73728 | tf_op args[1]
  0.9 1.0 %copy.8.feat_hbm = bf16[128,440]{1,0:T(8,128)(2,1)S(1)} copy(bf16[128,440]{0,1:T(8,128)(2,1)} %param.3) | data formatting | bytes 225280 | tf_op args[0]
  1.9 0.0 copy-start
  1.9 42.3 %ridge.1 = f32[128,144]{1,0:T(8,128)S(1)} custom-call(bf16[128,440]{1,0:T(8,128)(2,1)S(1)} %copy.8.feat_hbm, bf16[128,144]{1,0:T(8,128)(2,1)S(1)} %copy.9.coef_hbm), custom_call_target="tpu_custom_call" | custom-call | tf_op jit(solution)/shard_map/ridge/pallas_call | solution.py:261
  44.2 0.0 copy-done
  44.2 0.1 copy.10
  44.4 0.7 %copy.11 = f32[128,144]{0,1:T(8,128)} copy(f32[128,144]{1,0:T(8,128)S(1)} %sub.3) | data formatting | bytes 147456 | tf_op jit(solution)/shard_map/sub | solution.py:285
  (1 shorter events, 0.0 us)
Async XLA Ops:
  1.9 42.3 %copy-start = (f32[128,144]{0,1:T(8,128)S(1)}, f32[128,144]{0,1:T(8,128)}, u32[]{:S(2)}) copy-start(f32[128,144]{0,1:T(8,128)} %param.5) | copy-start | bytes 221188

commit v2 on v1

--- a/solution.py
+++ b/solution.py
@@ -28,7 +28,7 @@
 
 def kernel(
     feat_hbm, coef_hbm, out_ref,
-    feat, coef, cols, weights, rows, gram, sent, inbox, own_sum,
+    feat, coef, cols, weights, rows, gram, sums, sent, inbox, own_sum,
     load_sem, z_send, z_recv, chip_send, chip_recv, p_send, q_send, relay_send, row_recv, out_send, out_recv,
 ):
     row, col = lax.axis_index("row"), lax.axis_index("col")
@@ -64,29 +64,22 @@
     load_feat.wait()
     load_coef.wait()
 
-    low = feat[:, 0:384].astype(jnp.float32)
-    high = feat[:, 384:FEAT].astype(jnp.float32)
-    square = jnp.sum(low * low, axis=1, keepdims=True) + jnp.sum(high * high, axis=1, keepdims=True)
+    values = feat[...].astype(jnp.float32)
+    head = coef[0:HEAD, :].astype(jnp.float32)
+    square = jnp.sum(values * values, axis=0, keepdims=True)
     first = square.astype(jnp.bfloat16).astype(jnp.float32)
     second = (square - first).astype(jnp.bfloat16).astype(jnp.float32)
     third = square - first - second
-    lane = lax.broadcasted_iota(jnp.int32, (OWN, 128), 1)
-    high = jnp.concatenate([high, jnp.zeros((OWN, 128 - high.shape[1]), jnp.float32)], axis=1)
-    coef_low = coef[:, 0:128].astype(jnp.float32)
-    coef_high = jnp.concatenate([coef[:, 128:OUTS].astype(jnp.float32), jnp.zeros((OWN, 256 - OUTS), jnp.float32)], axis=1)
-    pieces = jnp.where(lane % 3 == 2, first, jnp.where(lane % 3 == 0, second, third))
-    ones = jnp.ones((OWN, 128), jnp.float32)
-    nothing = jnp.zeros((OWN, 128), jnp.float32)
-    column_tail = jnp.where(lane < 56, high * -2.0, jnp.where(lane < 59, pieces, jnp.where(lane < 62, ones, nothing)))
-    column_tail = jnp.where(lane < 64, column_tail, pltpu.roll(coef_low, 64, 1))
-    row_tail = jnp.where(lane < 56, high, jnp.where(lane < 59, ones, jnp.where(lane < 62, pieces, nothing)))
-    cols[0, :, 0:384] = (low * -2.0).astype(jnp.bfloat16)
-    cols[0, :, 384:PAD] = column_tail.astype(jnp.bfloat16)
-    for t in range(3):
-        rows[0, t * 128 : (t + 1) * 128, :] = jnp.transpose(low[:, t * 128 : (t + 1) * 128]).astype(jnp.bfloat16)
-    rows[0, 384:PAD, :] = jnp.transpose(row_tail).astype(jnp.bfloat16)
-    weights[0, 0:128, :] = jnp.transpose(coef_low).astype(jnp.bfloat16)
-    weights[0, 128:OUTS, :] = jnp.transpose(coef_high)[0 : OUTS - 128].astype(jnp.bfloat16)
+    at = lax.broadcasted_iota(jnp.int32, (8, OWN), 0)
+    pieces = jnp.where(at % 3 == 0, first, jnp.where(at % 3 == 1, second, third))
+    column_extra = jnp.where(at < 3, pieces, jnp.where(at < 6, 1.0, 0.0))
+    row_extra = jnp.where(at < 3, 1.0, jnp.where(at < 6, pieces, 0.0))
+    by_rows = jnp.concatenate([values, row_extra, jnp.zeros_like(head)], axis=0)
+    rows[0] = by_rows.astype(jnp.bfloat16)
+    by_columns = jnp.concatenate([values * -2.0, column_extra, head], axis=0)
+    for t in range(4):
+        cols[0, :, t * 128 : (t + 1) * 128] = jnp.transpose(by_columns[t * 128 : (t + 1) * 128]).astype(jnp.bfloat16)
+    weights[0] = coef[...]
 
     pl.semaphore_wait(barrier, len(near))
 
@@ -201,17 +194,37 @@
         from_sibling(dz)
         head_rows(2 * dz)
         head_rows(2 * dz + 1)
-    for piece in range(5):
+
+    def against(b, distances):
+        group = jnp.concatenate([rows[4 * b + a] for a in range(4)], axis=1)
+        for at, dz in enumerate(distances):
+            block = cols[2 * dz : 2 * dz + 2].reshape(2 * OWN, PAD)
+            gram[2 * at * OWN : 2 * (at + 1) * OWN, :] = laplacian(contract(block, group))
+        factors = jnp.concatenate([weights[2 * dz + half] for dz in distances for half in range(2)], axis=1)
+        return contract(factors, gram[0 : 2 * len(distances) * OWN, :])
+
+    near_columns, far_columns = (0, 1, 7, 2, 6), (3, 5, 4)
+    for a, b in ((0, 1), (1, 1)):
+        row_arrived(a, b)
+
+    @pl.loop(0, 2)
+    def _(b):
+        sums[b] = against(b, near_columns)
+
+    for piece in (0, 2, 1, 3, 4):
         z_arrived(4, piece)
     to_sibling(4)
+    for a, b in ((3, 3), (2, 3), (0, 2), (1, 2), (2, 2), (3, 2)):
+        row_arrived(a, b)
+
+    @pl.loop(2, 4)
+    def _(b):
+        sums[b] = against(b, near_columns)
+
     for dz in (3, 5, 4):
         head_rows(2 * dz)
         from_sibling(dz)
         head_rows(2 * dz + 1)
-    for a, b in ((0, 1), (1, 1), (3, 3), (2, 3), (0, 2), (1, 2), (2, 2), (3, 2)):
-        row_arrived(a, b)
-
-    all_weights = jnp.concatenate([weights[slot] for slot in range(16)], axis=1)
 
     def out_copy(a, b):
         slot = 4 * b + a
@@ -222,11 +235,7 @@
 
     @pl.loop(0, 4)
     def _(b):
-        group = jnp.concatenate([rows[4 * b + a] for a in range(4)], axis=1)
-        for slot in range(0, 16, 2):
-            block = cols[slot : slot + 2].reshape(2 * OWN, PAD)
-            gram[slot * OWN : (slot + 2) * OWN, :] = laplacian(contract(block, group))
-        total = contract(all_weights, gram[...])
+        total = sums[b] + against(b, far_columns)
 
         @pl.when(b == 0)
         def _():
@@ -246,9 +255,7 @@
     for slot in range(1, 16):
         arrived(inbox.at[slot], out_recv.at[slot])
         total = total + inbox[slot].astype(jnp.float32)
-    out_ref[:, 0:128] = jnp.transpose(total[0:128])
-    rest = jnp.concatenate([total[128:OUTS], jnp.zeros((256 - OUTS, OWN), jnp.float32)], axis=0)
-    out_ref[:, 128:OUTS] = jnp.transpose(rest)[:, 0 : OUTS - 128]
+    out_ref[...] = total
 
     for copy in started:
         copy.wait_send()
@@ -260,16 +267,17 @@
     dma = pltpu.SemaphoreType.DMA
     predicted = pl.pallas_call(
         kernel,
-        out_shape=jax.ShapeDtypeStruct((OWN, OUTS), jnp.float32),
+        out_shape=jax.ShapeDtypeStruct((OUTS, OWN), jnp.float32),
         in_specs=[pl.BlockSpec(memory_space=pl.ANY)] * 2,
         out_specs=pl.BlockSpec(memory_space=pltpu.VMEM),
         scratch_shapes=[
-            pltpu.VMEM((OWN, FEAT), jnp.bfloat16),
-            pltpu.VMEM((OWN, OUTS), jnp.bfloat16),
+            pltpu.VMEM((FEAT, OWN), jnp.bfloat16),
+            pltpu.VMEM((OUTS, OWN), jnp.bfloat16),
             pltpu.VMEM((16, OWN, PAD), jnp.bfloat16),
             pltpu.VMEM((16, OUTS, OWN), jnp.bfloat16),
             pltpu.VMEM((16, PAD, OWN), jnp.bfloat16),
-            pltpu.VMEM((16 * OWN, 4 * OWN), jnp.bfloat16),
+            pltpu.VMEM((10 * OWN, 4 * OWN), jnp.bfloat16),
+            pltpu.VMEM((4, OUTS, 4 * OWN), jnp.float32),
             pltpu.VMEM((16, OUTS, OWN), jnp.bfloat16),
             pltpu.VMEM((16, OUTS, OWN), jnp.bfloat16),
             pltpu.VMEM((OUTS, OWN), jnp.float32),
@@ -279,10 +287,10 @@
             dma((4,)), dma((2, 4)), dma((4,)), dma((16,)),
             dma((16,)), dma((16,)),
         ],
-        compiler_params=pltpu.CompilerParams(collective_id=0, has_side_effects=True, vmem_limit_bytes=48 << 20),
+        compiler_params=pltpu.CompilerParams(collective_id=0, has_side_effects=True, vmem_limit_bytes=60 << 20),
         name="ridge",
-    )(features, coeffs)
-    return predicted - targets
+    )(features.T, coeffs.T)
+    return predicted.T - targets
 
 
 def solution(mesh):

time: 45.3 us -> 43.5 us (0.960)
  local copies, waits for them, and re-layouts: 2.73 us -> 0.01 us
  other arithmetic: 0.02 us -> 1.53 us
    unnamed x5 -> x2, local copies, waits for them, and re-layouts: 2 us -> 0.01 us
    sub x1, other arithmetic: 0.02 us -> 1.53 us  [per_device(): return predicted.T - targets]
    sub x1 -> x0, local copies, waits for them, and re-layouts: 0.73 us -> none  [per_device(): return predicted - targets]
where the time goes in v2:
time: 43.5 us; the launch traced here: 43.4 us
  Pallas kernels  41.9 us (96%)
  other arithmetic  1.53 us (4%)
    pallas_call x1, Pallas kernels, per_device(): pl.pallas_call(kernel, out_shape=jax.ShapeDtypeStruct((OUTS, OWN), jnp.fl...  41.9 us
    sub x1, other arithmetic, per_device(): return predicted.T - targets  1.53 us

profile of v2, /device:TPU:1, one launch (start us, length us, event | category | flops | bytes accessed | tf_op | source)
XLA Modules:
  0.0 43.4 jit_solution(10363233217456812333)
XLA Ops:
  0.0 0.0 copy-start
  0.0 41.9 %ridge.1 = f32[144,128]{1,0:T(8,128)} custom-call(bf16[440,128]{1,0:T(8,128)(2,1)} %bitcast.4, bf16[144,128]{1,0:T(8,128)(2,1)} %bitcast.5), custom_call_target="tpu_custom_call" | custom-call | tf_op jit(solution)/shard_map/ridge/pallas_call | solution.py:268
  41.9 0.0 copy-done
  41.9 1.5 %bitcast_subtract_fusion = f32[128,144]{0,1:T(8,128)} fusion(f32[128,144]{0,1:T(8,128)S(1)} %copy-done, f32[144,128]{1,0:T(8,128)} %ridge.1), kind=kLoop, calls=%fused_computation | loop fusion | flops 18432 | bytes 221184 | tf_op jit(solution)/shard_map/sub | solution.py:293
Async XLA Ops:
  0.0 41.9 %copy-start = (f32[128,144]{0,1:T(8,128)S(1)}, f32[128,144]{0,1:T(8,128)}, u32[]{:S(2)}) copy-start(f32[128,144]{0,1:T(8,128)} %param.5) | copy-start | bytes 221188

commit v3 on v2

--- a/solution.py
+++ b/solution.py
@@ -28,7 +28,7 @@
 
 def kernel(
     feat_hbm, coef_hbm, out_ref,
-    feat, coef, cols, weights, rows, gram, sums, sent, inbox, own_sum,
+    feat, coef, cols, weights, rows, gram, sums, sent, inbox,
     load_sem, z_send, z_recv, chip_send, chip_recv, p_send, q_send, relay_send, row_recv, out_send, out_recv,
 ):
     row, col = lax.axis_index("row"), lax.axis_index("col")
@@ -147,54 +147,6 @@
         tail = jnp.transpose(cols[slot, :, 384:PAD].astype(jnp.float32))
         weights[slot, 0:HEAD, :] = tail[HEAD:128].astype(jnp.bfloat16)
 
-    for piece in range(PIECES):
-        for up in (True, False):
-            z_hop(1, piece, up)
-        if piece == 0:
-            for a in (1, 3):
-                send_row(0, 0, a, 0, p_send.at[a])
-            across(0)
-            send_row(0, 0, 2, 0, p_send.at[2])
-    to_sibling(0)
-
-    def z_round(step, pieces):
-        for piece in pieces:
-            for up in (True, False):
-                z_arrived(8 - step if up else step, piece)
-                if step < 3 or (step == 3 and (piece < 2) == up):
-                    z_hop(step + 1, piece, up)
-
-    z_round(1, (0, 1, 2))
-    for a in (1, 3):
-        row_arrived(a, 0)
-        across(a)
-    relay(0)
-    z_round(1, (3, 4))
-    to_sibling(1)
-    to_sibling(7)
-    row_arrived(2, 0)
-    across(2)
-    z_round(2, (0, 1))
-    relay(1)
-    relay(3)
-    z_round(2, (2, 3, 4))
-    to_sibling(2)
-    to_sibling(6)
-    relay(2)
-    from_sibling(0)
-    for dz in (1, 7):
-        from_sibling(dz)
-        head_rows(2 * dz)
-        head_rows(2 * dz + 1)
-    head_rows(1)
-    z_round(3, range(5))
-    to_sibling(3)
-    to_sibling(5)
-    for dz in (2, 6):
-        from_sibling(dz)
-        head_rows(2 * dz)
-        head_rows(2 * dz + 1)
-
     def against(b, distances):
         group = jnp.concatenate([rows[4 * b + a] for a in range(4)], axis=1)
         for at, dz in enumerate(distances):
@@ -203,23 +155,71 @@
         factors = jnp.concatenate([weights[2 * dz + half] for dz in distances for half in range(2)], axis=1)
         return contract(factors, gram[0 : 2 * len(distances) * OWN, :])
 
+    for piece in range(PIECES):
+        for up in (True, False):
+            z_hop(1, piece, up)
+    for a in (1, 3):
+        send_row(0, 0, a, 0, p_send.at[a])
+    send_row(0, 0, 2, 0, p_send.at[2])
+    across(0)
+    to_sibling(0)
+
+    def z_round(step, pieces):
+        for piece in pieces:
+            for up in (True, False):
+                z_arrived(8 - step if up else step, piece)
+                if step < 3 or (step == 3 and (piece < 2) == up):
+                    z_hop(step + 1, piece, up)
+
+    z_round(1, range(5))
+    to_sibling(1)
+    to_sibling(7)
+    for a in (1, 3):
+        row_arrived(a, 0)
+        across(a)
+    relay(0)
+    z_round(2, (0, 1))
+    row_arrived(2, 0)
+    across(2)
+    z_round(2, (2,))
+    from_sibling(0)
+    head_rows(1)
+    sums[0] = against(0, (0,))
+    z_round(2, (3, 4))
+    to_sibling(2)
+    to_sibling(6)
+    for dz in (1, 7):
+        from_sibling(dz)
+        head_rows(2 * dz)
+        head_rows(2 * dz + 1)
+    z_round(3, (0,))
+    sums[0] += against(0, (1,))
+    z_round(3, (1,))
+    sums[0] += against(0, (7,))
+    z_round(3, (2,3, 4))
+    relay(1)
+    relay(3)
+    relay(2)
+    to_sibling(3)
+    to_sibling(5)
+    for dz in (2, 6):
+        from_sibling(dz)
+        head_rows(2 * dz)
+        head_rows(2 * dz + 1)
+
     near_columns, far_columns = (0, 1, 7, 2, 6), (3, 5, 4)
     for a, b in ((0, 1), (1, 1)):
         row_arrived(a, b)
 
-    @pl.loop(0, 2)
-    def _(b):
-        sums[b] = against(b, near_columns)
+    sums[0] += against(0, (2, 6))
+    sums[1] = against(1, near_columns)
 
     for piece in (0, 2, 1, 3, 4):
         z_arrived(4, piece)
     to_sibling(4)
-    for a, b in ((3, 3), (2, 3), (0, 2), (1, 2), (2, 2), (3, 2)):
+    for a, b in ((3, 3), (2, 3)):
         row_arrived(a, b)
-
-    @pl.loop(2, 4)
-    def _(b):
-        sums[b] = against(b, near_columns)
+    sums[3] = against(3, near_columns)
 
     for dz in (3, 5, 4):
         head_rows(2 * dz)
@@ -233,25 +233,23 @@
             device_id=plane(a, b), device_id_type=MESH,
         )
 
-    @pl.loop(0, 4)
-    def _(b):
-        total = sums[b] + against(b, far_columns)
-
-        @pl.when(b == 0)
-        def _():
-            own_sum[...] = total[:, 0:OWN]
-
-        for a in range(4):
+    def hand_out(b, total, first):
+        for a in range(first, 4):
             sent[4 * b + a] = total[:, a * OWN : (a + 1) * OWN].astype(jnp.bfloat16)
-        for a in range(4):
-            if a == 0:
-                @pl.when(b > 0)
-                def _():
-                    out_copy(0, b).start()
-            else:
-                out_copy(a, b).start()
-
-    total = own_sum[...]
+        for a in range(first, 4):
+            out_copy(a, b).start()
+
+    @pl.loop(0, 2)
+    def _(turn):
+        b = 2 * turn + 1
+        hand_out(b, sums[b] + against(b, far_columns), 0)
+
+    for a in range(4):
+        row_arrived(a, 2)
+    hand_out(2, against(2, near_columns + far_columns), 0)
+    total = sums[0] + against(0, far_columns)
+    hand_out(0, total, 1)
+    total = total[:, 0:OWN]
     for slot in range(1, 16):
         arrived(inbox.at[slot], out_recv.at[slot])
         total = total + inbox[slot].astype(jnp.float32)
@@ -276,20 +274,19 @@
             pltpu.VMEM((16, OWN, PAD), jnp.bfloat16),
             pltpu.VMEM((16, OUTS, OWN), jnp.bfloat16),
             pltpu.VMEM((16, PAD, OWN), jnp.bfloat16),
-            pltpu.VMEM((10 * OWN, 4 * OWN), jnp.bfloat16),
+            pltpu.VMEM((16 * OWN, 4 * OWN), jnp.bfloat16),
             pltpu.VMEM((4, OUTS, 4 * OWN), jnp.float32),
             pltpu.VMEM((16, OUTS, OWN), jnp.bfloat16),
             pltpu.VMEM((16, OUTS, OWN), jnp.bfloat16),
-            pltpu.VMEM((OUTS, OWN), jnp.float32),
             dma((2,)),
             dma((2, 4, PIECES)), dma((8, PIECES)),
             dma((8, 2)), dma((8, 2)),
             dma((4,)), dma((2, 4)), dma((4,)), dma((16,)),
             dma((16,)), dma((16,)),
         ],
-        compiler_params=pltpu.CompilerParams(collective_id=0, has_side_effects=True, vmem_limit_bytes=60 << 20),
+        compiler_params=pltpu.CompilerParams(collective_id=0, has_side_effects=True, vmem_limit_bytes=32 << 20),
         name="ridge",
-    )(features.T, coeffs.T)
+    )(pltpu.with_memory_space_constraint(features.T, pltpu.HBM), pltpu.with_memory_space_constraint(coeffs.T, pltpu.HBM))
     return predicted.T - targets
 
 

time: 43.5 us -> 39.2 us (0.901)
  Pallas kernels: 41.9 us -> 38.4 us
  other arithmetic: 1.53 us -> 0.64 us
    pallas_call x1, Pallas kernels: 41.9 us -> 38.4 us  [per_device(): pl.pallas_call(kernel, out_shape=jax.ShapeDtypeStruct((OUTS, OWN), jnp.fl...]
    sub x1, other arithmetic: 1.53 us -> 0.64 us  [per_device(): return predicted.T - targets]
where the time goes in v3:
time: 39.2 us; the launch traced here: 39.1 us
  Pallas kernels  38.4 us (98%)
  other arithmetic  0.64 us (2%)
    pallas_call x1, Pallas kernels, per_device(): pl.pallas_call(kernel, out_shape=jax.ShapeDtypeStruct((OUTS, OWN), jnp.fl...  38.4 us

profile of v3, /device:TPU:1, one launch (start us, length us, event | category | flops | bytes accessed | tf_op | source)
XLA Modules:
  0.0 39.1 jit_solution(8611371154303579422)
XLA Ops:
  0.0 0.0 copy-start
  0.0 38.4 %ridge.1 = f32[144,128]{1,0:T(8,128)S(1)} custom-call(bf16[440,128]{1,0:T(8,128)(2,1)} %bitcast.4, bf16[144,128]{1,0:T(8,128)(2,1)} %bitcast.5), custom_call_target="tpu_custom_call" | custom-call | tf_op jit(solution)/shard_map/ridge/pallas_call | solution.py:266
  38.5 0.0 copy-done
  38.5 0.6 %bitcast_subtract_fusion = f32[128,144]{0,1:T(8,128)} fusion(f32[128,144]{0,1:T(8,128)S(1)} %copy-done, f32[144,128]{1,0:T(8,128)S(1)} %ridge.1), kind=kLoop, calls=%fused_computation | loop fusion | flops 18432 | bytes 221184 | tf_op jit(solution)/shard_map/sub | solution.py:290
Async XLA Ops:
  0.0 38.5 %copy-start = (f32[128,144]{0,1:T(8,128)S(1)}, f32[128,144]{0,1:T(8,128)}, u32[]{:S(2)}) copy-start(f32[128,144]{0,1:T(8,128)} %param.5) | copy-start | bytes 221188

commit v4 on v3

--- a/solution.py
+++ b/solution.py
@@ -15,6 +15,13 @@
 HEAD = 64
 PIECES = 5
 LOG2E = 1.4426950408889634
+PLACES = (
+    (0, 0), (1, 0), (2, 0), (3, 0),
+    (0, 1), (1, 1), (0, 3), (3, 3),
+    (2, 1), (3, 1), (2, 3), (1, 3),
+    (0, 2), (1, 2), (2, 2), (3, 2),
+)
+SLOT = {place: slot for slot, place in enumerate(PLACES)}
 
 
 def contract(a, b):
@@ -28,7 +35,7 @@
 
 def kernel(
     feat_hbm, coef_hbm, out_ref,
-    feat, coef, cols, weights, rows, gram, sums, sent, inbox,
+    feat, coef, cols, weights, rows, gram, first_sums, sums, sent, inbox,
     load_sem, z_send, z_recv, chip_send, chip_recv, p_send, q_send, relay_send, row_recv, out_send, out_recv,
 ):
     row, col = lax.axis_index("row"), lax.axis_index("col")
@@ -122,14 +129,14 @@
         arrived(part(2 * dz + 1, 4), chip_recv.at[dz, 1])
 
     def row_block(a, b):
-        return rows.at[4 * b + a, pl.ds(0, WIRE), :]
+        return rows.at[SLOT[a, b], pl.ds(0, WIRE), :]
 
     def send_row(a, b, to_a, to_b, send_sem):
         there = ((a - to_a) % 4, (b - to_b) % 4)
-        send(row_block(a, b), row_block(*there), send_sem, row_recv.at[4 * there[1] + there[0]], plane(to_a, to_b))
+        send(row_block(a, b), row_block(*there), send_sem, row_recv.at[SLOT[there]], plane(to_a, to_b))
 
     def row_arrived(a, b):
-        arrived(row_block(a, b), row_recv.at[4 * b + a])
+        arrived(row_block(a, b), row_recv.at[SLOT[a, b]])
 
     def across(a):
         send_row(a, 0, 0, 1, q_send.at[0, a])
@@ -147,8 +154,8 @@
         tail = jnp.transpose(cols[slot, :, 384:PAD].astype(jnp.float32))
         weights[slot, 0:HEAD, :] = tail[HEAD:128].astype(jnp.bfloat16)
 
-    def against(b, distances):
-        group = jnp.concatenate([rows[4 * b + a] for a in range(4)], axis=1)
+    def against(group, distances):
+        group = jnp.concatenate([rows[4 * group + i] for i in range(4)], axis=1)
         for at, dz in enumerate(distances):
             block = cols[2 * dz : 2 * dz + 2].reshape(2 * OWN, PAD)
             gram[2 * at * OWN : 2 * (at + 1) * OWN, :] = laplacian(contract(block, group))
@@ -184,7 +191,7 @@
     z_round(2, (2,))
     from_sibling(0)
     head_rows(1)
-    sums[0] = against(0, (0,))
+    first_sums[...] = against(0, (0,))
     z_round(2, (3, 4))
     to_sibling(2)
     to_sibling(6)
@@ -193,64 +200,61 @@
         head_rows(2 * dz)
         head_rows(2 * dz + 1)
     z_round(3, (0,))
-    sums[0] += against(0, (1,))
+    first_sums[...] += against(0, (1,))
     z_round(3, (1,))
-    sums[0] += against(0, (7,))
-    z_round(3, (2,3, 4))
+    first_sums[...] += against(0, (7,))
+    z_round(3, (2, 3, 4))
+    to_sibling(3)
+    to_sibling(5)
     relay(1)
     relay(3)
     relay(2)
-    to_sibling(3)
-    to_sibling(5)
     for dz in (2, 6):
         from_sibling(dz)
         head_rows(2 * dz)
         head_rows(2 * dz + 1)
 
     near_columns, far_columns = (0, 1, 7, 2, 6), (3, 5, 4)
-    for a, b in ((0, 1), (1, 1)):
-        row_arrived(a, b)
-
-    sums[0] += against(0, (2, 6))
-    sums[1] = against(1, near_columns)
+    row_arrived(0, 1)
+    row_arrived(1, 1)
+    row_arrived(3, 3)
+
+    sums[...] = against(1, near_columns)
 
     for piece in (0, 2, 1, 3, 4):
         z_arrived(4, piece)
     to_sibling(4)
-    for a, b in ((3, 3), (2, 3)):
-        row_arrived(a, b)
-    sums[3] = against(3, near_columns)
-
-    for dz in (3, 5, 4):
+    for dz in (3, 5):
         head_rows(2 * dz)
         from_sibling(dz)
         head_rows(2 * dz + 1)
-
-    def out_copy(a, b):
-        slot = 4 * b + a
+    sums[...] += against(1, (3, 5))
+    head_rows(8)
+    from_sibling(4)
+    head_rows(9)
+
+    def out_copy(slot):
         return pltpu.make_async_remote_copy(
             src_ref=sent.at[slot], dst_ref=inbox.at[slot], send_sem=out_send.at[slot], recv_sem=out_recv.at[slot],
-            device_id=plane(a, b), device_id_type=MESH,
+            device_id=plane(*PLACES[slot]), device_id_type=MESH,
         )
 
-    def hand_out(b, total, first):
-        for a in range(first, 4):
-            sent[4 * b + a] = total[:, a * OWN : (a + 1) * OWN].astype(jnp.bfloat16)
-        for a in range(first, 4):
-            out_copy(a, b).start()
-
-    @pl.loop(0, 2)
-    def _(turn):
-        b = 2 * turn + 1
-        hand_out(b, sums[b] + against(b, far_columns), 0)
-
+    def hand_out(group, total, first):
+        for i in range(first, 4):
+            sent[4 * group + i] = total[:, i * OWN : (i + 1) * OWN].astype(jnp.bfloat16)
+        for i in range(first, 4):
+            out_copy(4 * group + i).start()
+
+    hand_out(1, sums[...] + against(1, (4,)), 0)
+    row_arrived(2, 3)
+    hand_out(2, against(2, near_columns + far_columns), 0)
     for a in range(4):
         row_arrived(a, 2)
-    hand_out(2, against(2, near_columns + far_columns), 0)
-    total = sums[0] + against(0, far_columns)
+    hand_out(3, against(3, near_columns + far_columns), 0)
+    total = first_sums[...] + against(0, (2, 6) + far_columns)
     hand_out(0, total, 1)
     total = total[:, 0:OWN]
-    for slot in range(1, 16):
+    for slot in (*range(4, 16), 1, 3, 2):
         arrived(inbox.at[slot], out_recv.at[slot])
         total = total + inbox[slot].astype(jnp.float32)
     out_ref[...] = total
@@ -258,7 +262,7 @@
     for copy in started:
         copy.wait_send()
     for slot in range(1, 16):
-        out_copy(slot % 4, slot // 4).wait_send()
+        out_copy(slot).wait_send()
 
 
 def per_device(features, coeffs, targets):
@@ -275,7 +279,8 @@
             pltpu.VMEM((16, OUTS, OWN), jnp.bfloat16),
             pltpu.VMEM((16, PAD, OWN), jnp.bfloat16),
             pltpu.VMEM((16 * OWN, 4 * OWN), jnp.bfloat16),
-            pltpu.VMEM((4, OUTS, 4 * OWN), jnp.float32),
+            pltpu.VMEM((OUTS, 4 * OWN), jnp.float32),
+            pltpu.VMEM((OUTS, 4 * OWN), jnp.float32),
             pltpu.VMEM((16, OUTS, OWN), jnp.bfloat16),
             pltpu.VMEM((16, OUTS, OWN), jnp.bfloat16),
             dma((2,)),

time: 39.2 us -> 39 us (level)
  no operation moved by 1% of the time
where the time goes in v4:
time: 39 us; the launch traced here: 38.9 us
  Pallas kernels  38.3 us (98%)
  other arithmetic  0.64 us (2%)
    pallas_call x1, Pallas kernels, per_device(): pl.pallas_call(kernel, out_shape=jax.ShapeDtypeStruct((OUTS, OWN), jnp.fl...  38.3 us

profile of v4, /device:TPU:1, one launch (start us, length us, event | category | flops | bytes accessed | tf_op | source)
XLA Modules:
  0.0 38.9 jit_solution(13603618248579439905)
XLA Ops:
  0.0 0.0 copy-start
  0.0 38.3 %ridge.1 = f32[144,128]{1,0:T(8,128)S(1)} custom-call(bf16[440,128]{1,0:T(8,128)(2,1)} %bitcast.4, bf16[144,128]{1,0:T(8,128)(2,1)} %bitcast.5), custom_call_target="tpu_custom_call" | custom-call | tf_op jit(solution)/shard_map/ridge/pallas_call | solution.py:270
  38.3 0.0 copy-done
  38.3 0.6 %bitcast_subtract_fusion = f32[128,144]{0,1:T(8,128)} fusion(f32[128,144]{0,1:T(8,128)S(1)} %copy-done, f32[144,128]{1,0:T(8,128)S(1)} %ridge.1), kind=kLoop, calls=%fused_computation | loop fusion | flops 18432 | bytes 221184 | tf_op jit(solution)/shard_map/sub | solution.py:295
Async XLA Ops:
  0.0 38.3 %copy-start = (f32[128,144]{0,1:T(8,128)S(1)}, f32[128,144]{0,1:T(8,128)}, u32[]{:S(2)}) copy-start(f32[128,144]{0,1:T(8,128)} %param.5) | copy-start | bytes 221188

commit v5 on v4

--- a/solution.py
+++ b/solution.py
@@ -117,6 +117,9 @@
             z_send.at[int(up), step - 1, piece], z_recv.at[dst, piece], line(1 if up else -1),
         )
 
+    def in_turn(turn, up):
+        return turn if up else (turn + 2) % PIECES
+
     def z_arrived(dz, piece):
         arrived(part(2 * dz, piece), z_recv.at[dz, piece])
 
@@ -162,18 +165,19 @@
         factors = jnp.concatenate([weights[2 * dz + half] for dz in distances for half in range(2)], axis=1)
         return contract(factors, gram[0 : 2 * len(distances) * OWN, :])
 
-    for piece in range(PIECES):
+    for turn in range(PIECES):
         for up in (True, False):
-            z_hop(1, piece, up)
+            z_hop(1, in_turn(turn, up), up)
     for a in (1, 3):
         send_row(0, 0, a, 0, p_send.at[a])
     send_row(0, 0, 2, 0, p_send.at[2])
     across(0)
     to_sibling(0)
 
-    def z_round(step, pieces):
-        for piece in pieces:
+    def z_round(step, turns):
+        for turn in turns:
             for up in (True, False):
+                piece = in_turn(turn, up)
                 z_arrived(8 - step if up else step, piece)
                 if step < 3 or (step == 3 and (piece < 2) == up):
                     z_hop(step + 1, piece, up)
@@ -199,13 +203,8 @@
         from_sibling(dz)
         head_rows(2 * dz)
         head_rows(2 * dz + 1)
-    z_round(3, (0,))
-    first_sums[...] += against(0, (1,))
-    z_round(3, (1,))
-    first_sums[...] += against(0, (7,))
-    z_round(3, (2, 3, 4))
-    to_sibling(3)
-    to_sibling(5)
+    z_round(3, (0, 1, 2))
+    first_sums[...] += against(0, (1, 7))
     relay(1)
     relay(3)
     relay(2)
@@ -213,12 +212,14 @@
         from_sibling(dz)
         head_rows(2 * dz)
         head_rows(2 * dz + 1)
+    z_round(3, (3, 4))
+    to_sibling(3)
+    to_sibling(5)
 
     near_columns, far_columns = (0, 1, 7, 2, 6), (3, 5, 4)
     row_arrived(0, 1)
     row_arrived(1, 1)
     row_arrived(3, 3)
-
     sums[...] = against(1, near_columns)
 
     for piece in (0, 2, 1, 3, 4):

time: 39 us -> 38.2 us (0.979)
  Pallas kernels: 38.3 us -> 37.4 us
    pallas_call x1, Pallas kernels: 38.3 us -> 37.4 us  [per_device(): pl.pallas_call(kernel, out_shape=jax.ShapeDtypeStruct((OUTS, OWN), jnp.fl...]
where the time goes in v5:
time: 38.2 us; the launch traced here: 38.1 us
  Pallas kernels  37.4 us (98%)
  other arithmetic  0.64 us (2%)
    pallas_call x1, Pallas kernels, per_device(): pl.pallas_call(kernel, out_shape=jax.ShapeDtypeStruct((OUTS, OWN), jnp.fl...  37.4 us

profile of v5, /device:TPU:1, one launch (start us, length us, event | category | flops | bytes accessed | tf_op | source)
XLA Modules:
  0.0 38.1 jit_solution(3890991346011807391)
XLA Ops:
  0.0 0.0 copy-start
  0.0 37.4 %ridge.1 = f32[144,128]{1,0:T(8,128)S(1)} custom-call(bf16[440,128]{1,0:T(8,128)(2,1)} %bitcast.4, bf16[144,128]{1,0:T(8,128)(2,1)} %bitcast.5), custom_call_target="tpu_custom_call" | custom-call | tf_op jit(solution)/shard_map/ridge/pallas_call | solution.py:271
  37.4 0.0 copy-done
  37.5 0.6 %bitcast_subtract_fusion = f32[128,144]{0,1:T(8,128)} fusion(f32[128,144]{0,1:T(8,128)S(1)} %copy-done, f32[144,128]{1,0:T(8,128)S(1)} %ridge.1), kind=kLoop, calls=%fused_computation | loop fusion | flops 18432 | bytes 221184 | tf_op jit(solution)/shard_map/sub | solution.py:296
Async XLA Ops:
  0.0 37.4 %copy-start = (f32[128,144]{0,1:T(8,128)S(1)}, f32[128,144]{0,1:T(8,128)}, u32[]{:S(2)}) copy-start(f32[128,144]{0,1:T(8,128)} %param.5) | copy-start | bytes 221188

commit v6 on v5

--- a/solution.py
+++ b/solution.py
@@ -36,7 +36,7 @@
 def kernel(
     feat_hbm, coef_hbm, out_ref,
     feat, coef, cols, weights, rows, gram, first_sums, sums, sent, inbox,
-    load_sem, z_send, z_recv, chip_send, chip_recv, p_send, q_send, relay_send, row_recv, out_send, out_recv,
+    load_sem, z_send, z_recv, chip_send, chip_recv, p_send, q_send, relay_send, row_recv, out_send, out_recv, last_send, last_recv,
 ):
     row, col = lax.axis_index("row"), lax.axis_index("col")
     z, core = row // 4, row % 2
@@ -224,14 +224,15 @@
 
     for piece in (0, 2, 1, 3, 4):
         z_arrived(4, piece)
-    to_sibling(4)
+        send(part(8, piece), part(9, piece), last_send.at[piece], last_recv.at[piece], sibling)
     for dz in (3, 5):
         head_rows(2 * dz)
         from_sibling(dz)
         head_rows(2 * dz + 1)
     sums[...] += against(1, (3, 5))
     head_rows(8)
-    from_sibling(4)
+    for piece in range(PIECES):
+        arrived(part(9, piece), last_recv.at[piece])
     head_rows(9)
 
     def out_copy(slot):
@@ -289,6 +290,7 @@
             dma((8, 2)), dma((8, 2)),
             dma((4,)), dma((2, 4)), dma((4,)), dma((16,)),
             dma((16,)), dma((16,)),
+            dma((PIECES,)), dma((PIECES,)),
         ],
         compiler_params=pltpu.CompilerParams(collective_id=0, has_side_effects=True, vmem_limit_bytes=32 << 20),
         name="ridge",

time: 38.2 us -> 38.3 us (level)
  no operation moved by 1% of the time
where the time goes in v6:
time: 38.3 us; the launch traced here: 38.2 us
  Pallas kernels  37.5 us (98%)
  other arithmetic  0.64 us (2%)
    pallas_call x1, Pallas kernels, per_device(): pl.pallas_call(kernel, out_shape=jax.ShapeDtypeStruct((OUTS, OWN), jnp.fl...  37.5 us

profile of v6, /device:TPU:1, one launch (start us, length us, event | category | flops | bytes accessed | tf_op | source)
XLA Modules:
  0.0 38.2 jit_solution(7392646262526496726)
XLA Ops:
  0.0 0.0 copy-start
  0.0 37.5 %ridge.1 = f32[144,128]{1,0:T(8,128)S(1)} custom-call(bf16[440,128]{1,0:T(8,128)(2,1)} %bitcast.4, bf16[144,128]{1,0:T(8,128)(2,1)} %bitcast.5), custom_call_target="tpu_custom_call" | custom-call | tf_op jit(solution)/shard_map/ridge/pallas_call | solution.py:272
  37.5 0.0 copy-done
  37.5 0.6 %bitcast_subtract_fusion = f32[128,144]{0,1:T(8,128)} fusion(f32[128,144]{0,1:T(8,128)S(1)} %copy-done, f32[144,128]{1,0:T(8,128)S(1)} %ridge.1), kind=kLoop, calls=%fused_computation | loop fusion | flops 18432 | bytes 221184 | tf_op jit(solution)/shard_map/sub | solution.py:298
Async XLA Ops:
  0.0 37.5 %copy-start = (f32[128,144]{0,1:T(8,128)S(1)}, f32[128,144]{0,1:T(8,128)}, u32[]{:S(2)}) copy-start(f32[128,144]{0,1:T(8,128)} %param.5) | copy-start | bytes 221188
